TPU v7x, 32 devices: a whole 2x2x4 slice. The times are simulated.
32 devices in a mesh: dp: 16 (over z, x, core), tensor: 2 (over y).
Axes of the slice: x: 2, y: 2, z: 4, core: 2. Of those that a mesh axis runs over, the one named last changes fastest.
Arguments:
- tokens: bfloat16 [6144, 2048], P(('dp', 'tensor')), may hold values from -6 to 6
- attn_gain: bfloat16 [2048], P('dp'), may hold values from 0.5 to 1.5
- q_weight: bfloat16 [2048, 4096], P('dp', 'tensor'), may hold values from -0.125 to 0.125
- key_matrix: bfloat16 [2048, 512], P('dp', 'tensor'), may hold values from -0.125 to 0.125
- value_matrix: bfloat16 [2048, 512], P('dp', 'tensor'), may hold values from -0.125 to 0.125
- o_weight: bfloat16 [4096, 2048], P('tensor', 'dp'), may hold values from -0.75 to 0.75
- query_norm_gain: bfloat16 [128], P('dp'), may hold values from 0.5 to 1.5
- k_gain: bfloat16 [128], P('dp'), may hold values from 0.5 to 1.5
- ffn_gain: bfloat16 [2048], P('dp'), may hold values from 0.5 to 1.5
- router_weight: bfloat16 [2048, 32], P('dp'), may hold values from -0.024902344 to 0.024902344
- gate_weight: bfloat16 [32, 2048, 768], P('dp', None, 'tensor'), may hold values from -0.125 to 0.125
- up_weight: bfloat16 [32, 2048, 768], P('dp', None, 'tensor'), may hold values from -0.125 to 0.125
- down_weight: bfloat16 [32, 768, 2048], P('dp', 'tensor'), may hold values from -0.625 to 0.625
- expert_ids: int32 [6144, 8], P('dp'), may hold values from 0 to 31, all different within a row; in each aligned block of 384 rows (0 to 383, 384 to 767, ...) at most 120 rows name the same one
- cotangent: bfloat16 [6144, 2048], P(('dp', 'tensor')), may hold values from -6 to 6
Outputs:
- output: bfloat16 [6144, 2048], P(('dp', 'tensor'))
- tokens_grad: float32 [6144, 2048], P(('dp', 'tensor'))
- attn_gain_grad: float32 [2048], P('dp')
- q_weight_grad: float32 [2048, 4096], P('dp', 'tensor')
- k_weight_grad: float32 [2048, 512], P('dp', 'tensor')
- v_weight_grad: float32 [2048, 512], P('dp', 'tensor')
- o_weight_grad: float32 [4096, 2048], P('tensor', 'dp')
- q_gain_grad: float32 [128], P('dp')
- k_gain_grad: float32 [128], P('dp')
- ffn_gain_grad: float32 [2048], P('dp')
- router_weight_grad: float32 [2048, 32], P('dp')
- gate_weight_grad: float32 [32, 2048, 768], P('dp', None, 'tensor')
- up_weight_grad: float32 [32, 2048, 768], P('dp', None, 'tensor')
- down_weight_grad: float32 [32, 768, 2048], P('dp', 'tensor')
Inputs may be any that keep to these rules, and one draw needn't show every extreme that they name: `expert_ids`: each row names 8 different experts. Among the 384 tokens of one sequence (the rows of one device) no expert is named more than 120 times, a bound that some block reaches.
All inputs are finite; a program needn't handle non-finite values.
Results may differ from a plain program's by a relative error of at most 0.019.
Values may be sent and summed in bfloat16 or wider, within the bound.
No kernel may reach another device: no remote copies, remote signals or barrier semaphores. Data moves between devices by JAX's collectives and lax.ppermute only.
A program may use at most 320 MiB of HBM per device.

v0:
```python
from functools import partial

import jax
import jax.numpy as jnp
from jax import lax
from jax.sharding import PartitionSpec as P

HEAD_ENTRIES = 128
TOP = 8
EXP_DEV = 2
TOK_DEV = 192


EPSILON = 1e-06
ROPE_THETA = 1000000.0
EXACT_PRECISION = lax.Precision.HIGHEST


def root_mean_norm(value_rows, gain):
    return (
        value_rows
        * lax.rsqrt(jnp.mean(value_rows * value_rows, axis=-1, keepdims=True) + EPSILON)
        * gain
    )


def apply_rotary(value_rows, cosine_lookup, sine_lookup):
    half_size = value_rows.shape[-1] // 2
    first_half = value_rows[..., :half_size]
    second_half = value_rows[..., half_size:]
    return jnp.concatenate(
        [
            first_half * cosine_lookup - second_half * sine_lookup,
            second_half * cosine_lookup + first_half * sine_lookup,
        ],
        axis=-1,
    )


def rope_tables(length_tokens):
    half_size = HEAD_ENTRIES // 2
    inverse = ROPE_THETA ** (-(jnp.arange(half_size, dtype=jnp.float32) * 2.0 / HEAD_ENTRIES))
    angles = jnp.arange(length_tokens, dtype=jnp.float32)[:, None] * inverse[None, :]
    return (jnp.cos(angles)[:, None, :], jnp.sin(angles)[:, None, :])


def head_post(cosine_lookup, sine_lookup, query_unrotated, key_unrotated, query_norm_gain, k_gain):
    return (
        apply_rotary(root_mean_norm(query_unrotated, query_norm_gain), cosine_lookup, sine_lookup),
        apply_rotary(root_mean_norm(key_unrotated, k_gain), cosine_lookup, sine_lookup),
    )


def swiglu(gate_proj, up_proj):
    return jax.nn.silu(gate_proj) * up_proj


def gather_dense(
    attn_gain,
    q_weight,
    key_matrix,
    value_matrix,
    o_weight,
    query_norm_gain,
    k_gain,
    ffn_gain,
    router_weight,
):
    return (
        lax.all_gather(attn_gain, "dp", axis=0, tiled=True),
        lax.all_gather(q_weight, "dp", axis=0, tiled=True),
        lax.all_gather(key_matrix, "dp", axis=0, tiled=True),
        lax.all_gather(value_matrix, "dp", axis=0, tiled=True),
        lax.all_gather(o_weight, "dp", axis=1, tiled=True),
        lax.all_gather(query_norm_gain, "dp", axis=0, tiled=True),
        lax.all_gather(k_gain, "dp", axis=0, tiled=True),
        lax.all_gather(ffn_gain, "dp", axis=0, tiled=True),
        lax.all_gather(router_weight, "dp", axis=0, tiled=True),
    )


def slot_tables(expert_ids, experts, capacity):
    pair_count = expert_ids.shape[0] * expert_ids.shape[1]
    flat_ids = expert_ids.reshape(pair_count)
    onehot = (flat_ids[:, None] == jnp.arange(experts, dtype=jnp.int32)[None, :]).astype(
        jnp.float32
    )
    block_size = 16 * expert_ids.shape[1]
    blocks = onehot.reshape(pair_count // block_size, block_size, experts)
    strict_lower = (jnp.arange(block_size)[:, None] > jnp.arange(block_size)[None, :]).astype(
        jnp.float32
    )
    within = jnp.einsum("ab,nbe->nae", strict_lower, blocks, precision=EXACT_PRECISION)
    totals = jnp.sum(blocks, axis=1)
    offsets = jnp.cumsum(totals, axis=0) - totals
    ranked = jnp.sum((within + offsets[:, None, :]) * blocks, axis=2).reshape(pair_count)
    position = flat_ids * capacity + ranked.astype(jnp.int32)
    token_index = jnp.arange(pair_count, dtype=jnp.int32) // expert_ids.shape[1]
    return (position, token_index)


def on_device(
    tokens,
    attn_gain,
    q_weight,
    key_matrix,
    value_matrix,
    o_weight,
    query_norm_gain,
    k_gain,
    ffn_gain,
    router_weight,
    gate_weight,
    up_weight,
    down_weight,
    expert_ids,
    cotangent,
):
    dp_size = lax.axis_size("dp")
    own_rows = tokens.shape[0]
    begin_row = lax.axis_index("tensor") * own_rows
    experts = EXP_DEV * dp_size
    capacity = 10 * TOK_DEV * TOP // (4 * experts)
    gain_attn, full_q, full_k, full_v, full_o, gain_query, gain_key, gain_ffn, full_router = (
        gather_dense(
            attn_gain,
            q_weight,
            key_matrix,
            value_matrix,
            o_weight,
            query_norm_gain,
            k_gain,
            ffn_gain,
            router_weight,
        )
    )
    layer_in = lax.all_gather(tokens, "tensor", axis=0, tiled=True)
    seq_rows = layer_in.shape[0]
    residual = layer_in.astype(jnp.float32)
    attn_gain32 = gain_attn.astype(jnp.float32)
    normalized_input = root_mean_norm(residual, attn_gain32).astype(jnp.bfloat16)
    query_unrotated = jnp.dot(normalized_input, full_q, preferred_element_type=jnp.float32)
    key_unrotated = jnp.dot(normalized_input, full_k, preferred_element_type=jnp.float32)
    v_raw = jnp.dot(normalized_input, full_v, preferred_element_type=jnp.float32)
    query_heads = full_q.shape[1] // HEAD_ENTRIES
    key_heads = full_k.shape[1] // HEAD_ENTRIES
    group_width = query_heads // key_heads
    cosine_lookup, sine_lookup = rope_tables(seq_rows)
    post_fn = partial(head_post, cosine_lookup, sine_lookup)
    query_gain32 = gain_query.astype(jnp.float32)
    key_gain32 = gain_key.astype(jnp.float32)
    q_heads = query_unrotated.reshape(seq_rows, query_heads, HEAD_ENTRIES)
    k_heads = key_unrotated.reshape(seq_rows, key_heads, HEAD_ENTRIES)
    query_rows, keys_rot = post_fn(q_heads, k_heads, query_gain32, key_gain32)
    q_low = query_rows.astype(jnp.bfloat16).reshape(seq_rows, key_heads, group_width, HEAD_ENTRIES)
    k_low = keys_rot.astype(jnp.bfloat16)
    v_low = v_raw.astype(jnp.bfloat16).reshape(seq_rows, key_heads, HEAD_ENTRIES)
    causal = jnp.arange(seq_rows)[:, None] >= jnp.arange(seq_rows)[None, :]
    score_scale = HEAD_ENTRIES ** (-0.5)
    scores = (
        jnp.einsum("qhgd,khd->hgqk", q_low, k_low, preferred_element_type=jnp.float32) * score_scale
    )
    exponent = jnp.where(causal, jnp.exp(scores), 0.0)
    row_total = jnp.sum(exponent, axis=-1, keepdims=True)
    log_total = jnp.log(row_total)
    context = jnp.einsum(
        "hgqk,khd->qhgd",
        (exponent / row_total).astype(jnp.bfloat16),
        v_low,
        preferred_element_type=jnp.float32,
    )
    context = context.reshape(seq_rows, query_heads * HEAD_ENTRIES).astype(jnp.bfloat16)
    attn_part = jnp.dot(context, full_o, preferred_element_type=jnp.float32)
    attn_out = lax.psum(attn_part, "tensor")
    hidden = residual + attn_out
    ffn_gain32 = gain_ffn.astype(jnp.float32)
    ffn_in = root_mean_norm(hidden, ffn_gain32).astype(jnp.bfloat16)
    ffn_in32 = ffn_in.astype(jnp.float32)
    router32 = full_router.astype(jnp.float32)
    logits = jnp.dot(ffn_in32, router32, precision=EXACT_PRECISION)
    chosen = jnp.exp(jnp.take_along_axis(logits, expert_ids, axis=1))
    gates = chosen / jnp.sum(chosen, axis=1, keepdims=True)
    position, token_index = slot_tables(expert_ids, experts, capacity)
    pair_count = position.shape[0]
    source_rows = jnp.full((experts * capacity,), seq_rows, jnp.int32).at[position].set(token_index)
    slot_gate = (
        jnp.zeros((experts * capacity,), jnp.float32).at[position].set(gates.reshape(pair_count))
    )
    padded = jnp.concatenate([ffn_in, jnp.zeros((1, ffn_in.shape[1]), jnp.bfloat16)], axis=0)
    send_rows = padded[source_rows].reshape(dp_size, EXP_DEV, capacity, ffn_in.shape[1])
    received = lax.all_to_all(send_rows, "dp", split_axis=0, concat_axis=0, tiled=True)
    gate_proj = jnp.einsum(
        "secd,edf->secf", received, gate_weight, preferred_element_type=jnp.float32
    )
    up_proj = jnp.einsum("secd,edf->secf", received, up_weight, preferred_element_type=jnp.float32)
    activated = swiglu(gate_proj, up_proj).astype(jnp.bfloat16)
    expert_out = jnp.einsum(
        "secf,efd->secd", activated, down_weight, preferred_element_type=jnp.float32
    ).astype(jnp.bfloat16)
    returned = lax.all_to_all(expert_out, "dp", split_axis=0, concat_axis=0, tiled=True).reshape(
        experts * capacity, ffn_in.shape[1]
    )
    pair_rows = position.reshape(seq_rows, TOP)
    ffn_part = jnp.zeros(hidden.shape, jnp.float32)
    for column in range(TOP):
        ffn_part = ffn_part + gates[:, column : column + 1] * returned[pair_rows[:, column]].astype(
            jnp.float32
        )
    ffn_own = lax.psum_scatter(
        ffn_part.astype(jnp.bfloat16), "tensor", scatter_dimension=0, tiled=True
    ).astype(jnp.float32)
    hidden_own = lax.dynamic_slice_in_dim(hidden, begin_row, own_rows, 0)
    output = (hidden_own + ffn_own).astype(jnp.bfloat16)
    cot_rows = lax.all_gather(cotangent, "tensor", axis=0, tiled=True)
    grad_out = cot_rows.astype(jnp.float32)
    padded_grad = jnp.concatenate(
        [cot_rows, jnp.zeros((1, cot_rows.shape[1]), jnp.bfloat16)], axis=0
    )
    grad_send = (padded_grad[source_rows].astype(jnp.float32) * slot_gate[:, None]).astype(
        jnp.bfloat16
    )
    grad_send = grad_send.reshape(dp_size, EXP_DEV, capacity, cot_rows.shape[1])
    grad_recv = lax.all_to_all(grad_send, "dp", split_axis=0, concat_axis=0, tiled=True)
    grad_act = jnp.einsum(
        "secd,efd->secf", grad_recv, down_weight, preferred_element_type=jnp.float32
    )
    swiglu_value, swiglu_back = jax.vjp(swiglu, gate_proj, up_proj)
    grad_gate, grad_up = swiglu_back(grad_act)
    grad_gate = grad_gate.astype(jnp.bfloat16)
    grad_up = grad_up.astype(jnp.bfloat16)
    down_weight_grad = jnp.einsum(
        "secf,secd->efd", activated, grad_recv, preferred_element_type=jnp.float32
    )
    gate_weight_grad = jnp.einsum(
        "secd,secf->edf", received, grad_gate, preferred_element_type=jnp.float32
    )
    up_weight_grad = jnp.einsum(
        "secd,secf->edf", received, grad_up, preferred_element_type=jnp.float32
    )
    grad_inputs = jnp.einsum(
        "secf,edf->secd", grad_gate, gate_weight, preferred_element_type=jnp.float32
    ) + jnp.einsum("secf,edf->secd", grad_up, up_weight, preferred_element_type=jnp.float32)
    grad_back = lax.all_to_all(
        grad_inputs.astype(jnp.bfloat16), "dp", split_axis=0, concat_axis=0, tiled=True
    )
    grad_back = grad_back.reshape(experts * capacity, cot_rows.shape[1])
    grad_ffn = jnp.zeros(hidden.shape, jnp.float32)
    gate_columns = []
    for column in range(TOP):
        index_col = pair_rows[:, column]
        grad_ffn = grad_ffn + grad_back[index_col].astype(jnp.float32)
        gate_columns.append(
            jnp.einsum(
                "td,td->t", returned[index_col], cot_rows, preferred_element_type=jnp.float32
            )
        )
    gate_grads = jnp.stack(gate_columns, axis=1)
    grad_chosen = gates * (gate_grads - jnp.sum(gates * gate_grads, axis=1, keepdims=True))
    expert_onehot = (
        expert_ids[:, :, None] == jnp.arange(experts, dtype=jnp.int32)[None, None, :]
    ).astype(jnp.float32)
    grad_logits = jnp.einsum("tj,tje->te", grad_chosen, expert_onehot, precision=EXACT_PRECISION)
    grad_ffn = grad_ffn + jnp.dot(grad_logits, router32.T, precision=EXACT_PRECISION)
    router_part = jnp.dot(ffn_in32.T, grad_logits, precision=EXACT_PRECISION)
    ffn_back = lax.psum(grad_ffn, "tensor")
    norm_value, ffn_norm_back = jax.vjp(root_mean_norm, hidden, ffn_gain32)
    grad_hidden, ffn_gain_grad = ffn_norm_back(ffn_back)
    grad_hidden = grad_hidden + grad_out
    grad_attn = grad_hidden.astype(jnp.bfloat16)
    o_grad = jnp.dot(context.T, grad_attn, preferred_element_type=jnp.float32)
    grad_context = jnp.dot(grad_attn, full_o.T, preferred_element_type=jnp.float32).astype(
        jnp.bfloat16
    )
    grad_context = grad_context.reshape(seq_rows, key_heads, group_width, HEAD_ENTRIES)
    scores_again = (
        jnp.einsum("qhgd,khd->hgqk", q_low, k_low, preferred_element_type=jnp.float32) * score_scale
    )
    probs_again = jnp.where(causal, jnp.exp(scores_again - log_total), 0.0)
    grad_probs = jnp.einsum(
        "qhgd,khd->hgqk", grad_context, v_low, preferred_element_type=jnp.float32
    )
    values_grad = jnp.einsum(
        "hgqk,qhgd->khd",
        probs_again.astype(jnp.bfloat16),
        grad_context,
        preferred_element_type=jnp.float32,
    )
    row_dot = jnp.sum(probs_again * grad_probs, axis=-1, keepdims=True)
    grad_scores = (probs_again * (grad_probs - row_dot)).astype(jnp.bfloat16)
    grad_queries = (
        jnp.einsum("hgqk,khd->qhgd", grad_scores, k_low, preferred_element_type=jnp.float32)
        * score_scale
    )
    grad_keys = (
        jnp.einsum("hgqk,qhgd->khd", grad_scores, q_low, preferred_element_type=jnp.float32)
        * score_scale
    )
    post_value, post_back = jax.vjp(post_fn, q_heads, k_heads, query_gain32, key_gain32)
    q_raw_grad, k_raw_grad, q_gain_part, k_gain_part = post_back(
        (grad_queries.reshape(seq_rows, query_heads, HEAD_ENTRIES), grad_keys)
    )
    q_raw_low = q_raw_grad.reshape(seq_rows, query_heads * HEAD_ENTRIES).astype(jnp.bfloat16)
    k_raw_low = k_raw_grad.reshape(seq_rows, key_heads * HEAD_ENTRIES).astype(jnp.bfloat16)
    v_raw_low = values_grad.reshape(seq_rows, key_heads * HEAD_ENTRIES).astype(jnp.bfloat16)
    q_grad = jnp.dot(normalized_input.T, q_raw_low, preferred_element_type=jnp.float32)
    k_grad = jnp.dot(normalized_input.T, k_raw_low, preferred_element_type=jnp.float32)
    v_grad = jnp.dot(normalized_input.T, v_raw_low, preferred_element_type=jnp.float32)
    grad_normed = (
        jnp.dot(q_raw_low, full_q.T, preferred_element_type=jnp.float32)
        + jnp.dot(k_raw_low, full_k.T, preferred_element_type=jnp.float32)
        + jnp.dot(v_raw_low, full_v.T, preferred_element_type=jnp.float32)
    )
    attn_back, router_sum, q_gain_sum, k_gain_sum = (
        lax.psum(grad_normed.astype(jnp.bfloat16), "tensor").astype(jnp.float32),
        lax.psum(router_part.astype(jnp.bfloat16), "tensor").astype(jnp.float32),
        lax.psum(q_gain_part.astype(jnp.bfloat16), "tensor").astype(jnp.float32),
        lax.psum(k_gain_part.astype(jnp.bfloat16), "tensor").astype(jnp.float32),
    )
    attn_value, attn_norm_back = jax.vjp(root_mean_norm, residual, attn_gain32)
    grad_residual, attn_gain_grad = attn_norm_back(attn_back)
    grad_residual = grad_residual + grad_hidden
    tokens_grad = lax.dynamic_slice_in_dim(grad_residual, begin_row, own_rows, 0)
    (
        attn_gain_shard,
        q_shard,
        k_shard,
        v_shard,
        o_shard,
        q_gain_shard,
        k_gain_shard,
        ffn_gain_shard,
        router_shard,
    ) = (
        lax.psum_scatter(attn_gain_grad, "dp", scatter_dimension=0, tiled=True),
        lax.psum_scatter(q_grad, "dp", scatter_dimension=0, tiled=True),
        lax.psum_scatter(k_grad, "dp", scatter_dimension=0, tiled=True),
        lax.psum_scatter(v_grad, "dp", scatter_dimension=0, tiled=True),
        lax.psum_scatter(o_grad, "dp", scatter_dimension=1, tiled=True),
        lax.psum_scatter(q_gain_sum, "dp", scatter_dimension=0, tiled=True),
        lax.psum_scatter(k_gain_sum, "dp", scatter_dimension=0, tiled=True),
        lax.psum_scatter(ffn_gain_grad, "dp", scatter_dimension=0, tiled=True),
        lax.psum_scatter(router_sum, "dp", scatter_dimension=0, tiled=True),
    )
    return (
        output,
        tokens_grad,
        attn_gain_shard,
        q_shard,
        k_shard,
        v_shard,
        o_shard,
        q_gain_shard,
        k_gain_shard,
        ffn_gain_shard,
        router_shard,
        gate_weight_grad,
        up_weight_grad,
        down_weight_grad,
    )


def solution(mesh):
    placed = (
        P(("dp", "tensor"), None),
        P("dp"),
        P("dp", "tensor"),
        P("dp", "tensor"),
        P("dp", "tensor"),
        P("tensor", "dp"),
        P("dp"),
        P("dp"),
        P("dp"),
        P("dp", None),
        P("dp", None, "tensor"),
        P("dp", None, "tensor"),
        P("dp", "tensor", None),
        P("dp", None),
        P(("dp", "tensor"), None),
    )
    return jax.shard_map(
        on_device,
        mesh=mesh,
        in_specs=placed,
        out_specs=(
            P(("dp", "tensor"), None),
            P(("dp", "tensor"), None),
            P("dp"),
            P("dp", "tensor"),
            P("dp", "tensor"),
            P("dp", "tensor"),
            P("tensor", "dp"),
            P("dp"),
            P("dp"),
            P("dp"),
            P("dp", None),
            P("dp", None, "tensor"),
            P("dp", None, "tensor"),
            P("dp", "tensor", None),
        ),
        check_vma=False,
    )
```

profile of v0, /device:TPU:0, one launch (start us, length us, event | category | flops | bytes accessed | tf_op | source)
XLA Modules:
  0.0 3018.2 jit_solution(2163481323485437558)
XLA Ops:
  14.3 34.9 %all-reduce.13 = (bf16[128]{0:T(256)(128)(2,1)S(1)}, bf16[128]{0:T(256)(128)(2,1)S(1)}) all-reduce(bf16[128]{0:T(256)(128)(2,1)S(1)} %dynamic-update-slice.1, bf16[128]{0:T(256)(128)(2,1)S(1)} %dynamic-update-slice), channel_id=1, replica_groups=mesh['dp'=16,'tensor'=2] {'dp'}, use_global_device_ids=true, to_apply=%add.7 | all-reduce | flops 256 | bytes 1024
  50.3 17.3 all-gather
  87.5 31.1 %all-gather.11.cloned.1.call-done = bf16[2048,256]{1,0:T(8,128)(2,1)} async-done(((bf16[128,256]{1,0:T(8,128)(2,1)}), bf16[2048,256]{1,0:T(8,128)(2,1)}) %all-gather.11.cloned.1.call-update) | async-done | bytes 1048592 | tf_op jit(solution)/shard_map/all_gather | solution.py:73
  121.8 72.1 %all-gather.15.cloned.1.call-done = bf16[2048,2048]{1,0:T(8,128)(2,1)} async-done(((bf16[128,2048]{1,0:T(8,128)(2,1)}), bf16[2048,2048]{1,0:T(8,128)(2,1)}) %all-gather.15.cloned.1.call-update) | async-done | bytes 8388624 | tf_op jit(solution)/shard_map/all_gather | solution.py:71
  219.8 52.4 %all-gather.17.cloned.1.call-done = bf16[2048,2048]{1,0:T(8,128)(2,1)} async-done(((bf16[2048,128]{1,0:T(8,128)(2,1)}), bf16[2048,2048]{1,0:T(8,128)(2,1)}) %all-gather.17.cloned.1.call-update) | async-done | bytes 8388624 | tf_op jit(solution)/shard_map/all_gather | solution.py:74
  281.8 18.5 all-gather.1
  306.7 11.8 scatter_custom_fusion
  318.5 46.9 %all-reduce.20.cloned.1.call-done = f32[384,2048]{1,0:T(8,128)} async-done(((f32[384,2048]{1,0:T(8,128)}), f32[384,2048]{1,0:T(8,128)}) %all-reduce.20.cloned.1.call-update) | async-done | bytes 3145744 | tf_op jit(solution)/shard_map/psum | solution.py:174
  372.7 31.1 %gather_fusion = bf16[3840,2048]{1,0:T(8,128)(2,1)} fusion(bf16[385,2048]{1,0:T(8,128)(2,1)} %concatenate.23, s32[4096]{0:T(1024)S(1)} %pad_clamp_fusion), kind=kCustom, calls=%fused_computation | custom fusion | bytes 31472640 | tf_op jit(solution)/shard_map/gather | solution.py:190
  403.8 345.6 %all_to_all.20 = bf16[16,2,120,2048]{3,2,1,0:T(8,128)(2,1)S(1)} all-to-all(bf16[16,2,120,2048]{3,2,1,0:T(8,128)(2,1)} %bitcast.225), channel_id=1, replica_groups=mesh['dp'=16,'tensor'=2] {'dp'}, dimensions={0} | all-to-all | bytes 31457280 | tf_op jit(solution)/shard_map/all_to_all | solution.py:191
  765.4 15.3 fusion.21
  780.7 11.1 convert_bitcast_fusion
  791.8 13.5 copy.231
  814.1 301.4 %all_gather.42 = bf16[2048,32]{0,1:T(8,128)(2,1)S(1)} all-gather(bf16[128,32]{0,1:T(8,128)(2,1)} %param.24), channel_id=1, replica_groups=mesh['dp'=16,'tensor'=2] {'dp'}, dimensions={0}, use_global_device_ids=true | all-gather | bytes 139264 | tf_op jit(solution)/shard_map/all_gather | solution.py:78
  1119.2 31.3 %gather_fusion.9 = bf16[3840,2048]{1,0:T(8,128)(2,1)} fusion(bf16[385,2048]{1,0:T(8,128)(2,1)} %concatenate.24, s32[4096]{0:T(1024)S(1)} %copy-done.60), kind=kCustom, calls=%fused_computation.9 | custom fusion | bytes 31472640 | tf_op jit(solution)/shard_map/gather | solution.py:219
  1152.5 24.9 gather_fusion.18
  1177.7 12.6 gather_fusion.8
  1190.3 12.7 gather_fusion.7
  1203.0 12.6 gather_fusion.6
  1215.6 12.6 gather_fusion.5
  1228.2 13.0 gather_fusion.4
  1241.1 12.6 gather_fusion.3
  1253.7 12.8 gather_fusion.2
  1266.5 12.5 gather_fusion.1
  1286.0 11.9 scatter_custom_fusion.1
  1306.8 390.0 %all_to_all.21 = bf16[16,2,120,2048]{3,2,1,0:T(8,128)(2,1)} all-to-all(bf16[16,2,120,2048]{3,2,1,0:T(8,128)(2,1)S(1)} %fusion), channel_id=1, replica_groups=mesh['dp'=16,'tensor'=2] {'dp'}, dimensions={0} | all-to-all | bytes 31457280 | tf_op jit(solution)/shard_map/all_to_all | solution.py:223
  1696.8 17.2 fusion.20
  1714.0 17.0 fusion.50
  1731.0 19.1 fusion.1
  1750.1 13.5 copy.234
  1770.6 277.9 %all-to-all-done.3 = bf16[16,2,120,2048]{3,2,1,0:T(8,128)(2,1)} async-done(((bf16[16,2,120,2048]{3,2,1,0:T(8,128)(2,1)}), bf16[16,2,120,2048]{3,2,1,0:T(8,128)(2,1)}, u32[]{:S(2)}, u32[]{:S(2)}) %all-to-all-start.3) | async-done | bytes 15728672 | tf_op jit(solution)/shard_map/all_to_all | solution.py:243
  2048.4 11.9 gather_fusion.17
  2060.3 11.9 gather_fusion.16
  2072.2 12.7 gather_fusion.15
  2084.9 12.6 gather_fusion.14
  2097.5 12.6 gather_fusion.13
  2110.1 12.8 gather_fusion.12
  2122.8 12.6 gather_fusion.11
  2135.4 13.0 gather_fusion.10
  2159.8 143.3 %all-reduce.22.cloned.1.call-done = f32[384,2048]{1,0:T(8,128)} async-done(((f32[384,2048]{1,0:T(8,128)}), f32[384,2048]{1,0:T(8,128)}) %all-reduce.22.cloned.1.call-update) | async-done | bytes 3145744 | tf_op jit(solution)/shard_map/psum | solution.py:265
  2382.7 47.9 %all-reduce.24.cloned.1.call-done = (bf16[384,2048]{1,0:T(8,128)(2,1)}, bf16[2048,32]{0,1:T(8,128)(2,1)}) async-done(((bf16[384,2048]{1,0:T(8,128)(2,1)}, bf16[2048,32]{0,1:T(8,128)(2,1)}), (bf16[384,2048]{1,0:T(8,128)(2,1)}, bf16[2048,32]{0,1:T(8,128)(2,1)})) %all-reduce.24.cloned.1.call-update) | async-done | bytes 1703952 | tf_op jit(solution)/shard_map/psum | solution.py:314
  2463.1 12.1 fusion.27
  2475.2 14.0 convolution_bitcast_fusion
  2489.2 14.2 convolution_bitcast_fusion.1
  2511.2 60.4 %all-reduce.12 = (f32[2048]{0:T(1024)S(1)}, f32[128]{0:T(128)S(1)}, f32[128]{0:T(128)S(1)}, f32[2048]{0:T(1024)S(1)}) all-reduce(f32[2048]{0:T(1024)S(1)} %get-tuple-element.18, bf16[128]{0:T(256)(128)(2,1)S(1)} %get-tuple-element.52, bf16[128]{0:T(256)(128)(2,1)S(1)} %get-tuple-element.53, ...), channel_id=3, replica_groups=mesh['dp'=16,'tensor'=2] {'dp'}, use_global_device_ids=true, to_apply=%region_22.23.clone | all-reduce | flops 4352 | bytes 34304
  2584.5 65.1 %reduce-scatter.13.cloned.1.call-done = f32[128,256]{1,0:T(8,128)} async-done(((f32[2048,256]{1,0:T(8,128)}), f32[128,256]{1,0:T(8,128)}) %reduce-scatter.13.cloned.1.call-update) | async-done | bytes 131088 | tf_op jit(solution)/shard_map/reduce_scatter | solution.py:337
  2649.6 180.6 %reduce-scatter.15.cloned.1.call-done = f32[2048,128]{1,0:T(8,128)} async-done(((f32[2048,2048]{1,0:T(8,128)}), f32[2048,128]{1,0:T(8,128)}) %reduce-scatter.15.cloned.1.call-update) | async-done | bytes 1048592 | tf_op jit(solution)/shard_map/reduce_scatter | solution.py:338
  2830.2 181.0 %reduce-scatter.9.cloned.1.call-done = f32[128,2048]{1,0:T(8,128)} async-done(((f32[2048,2048]{1,0:T(8,128)}), f32[128,2048]{1,0:T(8,128)}) %reduce-scatter.9.cloned.1.call-update) | async-done | bytes 1048592 | tf_op jit(solution)/shard_map/reduce_scatter | solution.py:335
  (354 shorter events, 275.1 us)
Async XLA Ops:
  7.2 773.6 %copy-start = (bf16[2,384,2048]{2,1,0:T(8,128)(2,1)S(1)}, bf16[2,384,2048]{2,1,0:T(8,128)(2,1)}, u32[]{:S(2)}) copy-start(bf16[2,384,2048]{2,1,0:T(8,128)(2,1)} %param.27) | copy-start | bytes 9437188
  7.2 62.7 %all-gather.9.cloned.1.call-start = ((), (), s32[]{:S(2)}) async-start(), calls=%async_computation.10 | async-start | bytes 2359296 | tf_op jit(solution)/shard_map/all_gather | solution.py:137
  7.9 71.6 %all-gather.13.cloned.1.call-start = ((), (), s32[]{:S(2)}) async-start(), calls=%async_computation.12 | async-start | bytes 1114112 | tf_op jit(solution)/shard_map/all_gather | solution.py:72
  8.7 109.9 %all-gather.11.cloned.1.call-start = ((), (), s32[]{:S(2)}) async-start(), calls=%async_computation.11 | async-start | bytes 1114112 | tf_op jit(solution)/shard_map/all_gather | solution.py:73
  9.4 184.4 %all-gather.15.cloned.1.call-start = ((), (), s32[]{:S(2)}) async-start(), calls=%async_computation.13 | async-start | bytes 8912896 | tf_op jit(solution)/shard_map/all_gather | solution.py:71
  10.0 262.2 %all-gather.17.cloned.1.call-start = ((), (), s32[]{:S(2)}) async-start(), calls=%async_computation.14 | async-start | bytes 8912896 | tf_op jit(solution)/shard_map/all_gather | solution.py:74
  10.6 354.8 %all-reduce.20.cloned.1.call-start = ((), (), s32[]{:S(2)}) async-start(), calls=%async_computation.15 | async-start | bytes 6291456 | tf_op jit(solution)/shard_map/psum | solution.py:174
  67.7 126.2 %copy-start.55 = (f32[16,1,128]{2,1,0:T(1,128)}, f32[16,1,128]{2,1,0:T(1,128)S(1)}, u32[]{:S(2)}) copy-start(f32[16,1,128]{2,1,0:T(1,128)S(1)} %convert_element_type.279) | copy-start | bytes 24580
  72.2 121.6 %copy-start.64 = (f32[384]{0:T(512)}, f32[384]{0:T(512)S(1)}, u32[]{:S(2)}) copy-start(f32[384]{0:T(512)S(1)} %fusion.101) | copy-start | bytes 4612
  82.8 38.9 %copy-start.77 = (f32[384,2]{0,1:T(2,128)}, f32[384,2]{0,1:T(2,128)S(1)}, u32[]{:S(2)}) copy-start(f32[384,2]{0,1:T(2,128)S(1)} %get-tuple-element.81) | copy-start | bytes 9220
  84.0 37.8 %copy-start.22 = (f32[384,2,128]{2,0,1:T(8,128)}, f32[384,2,128]{2,0,1:T(8,128)S(1)}, u32[]{:S(2)}) copy-start(f32[384,2,128]{2,0,1:T(8,128)S(1)} %copy.219) | copy-start | bytes 1179652
  281.2 19.8 copy-start.52
  306.6 61.6 %copy-start.79 = (s32[3072,1]{0,1:T(1,128)}, s32[3072,1]{0,1:T(1,128)S(1)}, u32[]{:S(2)}) copy-start(s32[3072,1]{0,1:T(1,128)S(1)} %compare_select_fusion.8) | copy-start | bytes 36868
  318.5 54.2 %copy-start.59 = (s32[4096]{0:T(1024)}, s32[4096]{0:T(1024)S(1)}, u32[]{:S(2)}) copy-start(s32[4096]{0:T(1024)S(1)} %pad_clamp_fusion) | copy-start | bytes 49156
  318.5 51.4 %copy-start.61 = (f32[16,1,128]{2,1,0:T(1,128)S(1)}, f32[16,1,128]{2,1,0:T(1,128)}, u32[]{:S(2)}) copy-start(f32[16,1,128]{2,1,0:T(1,128)} %convert_element_type.280) | copy-start | bytes 24580
  403.8 351.1 %copy-start.33 = (bf16[2,2048,384]{2,1,0:T(8,128)(2,1)S(1)}, bf16[2,2048,384]{2,1,0:T(8,128)(2,1)}, u32[]{:S(2)}) copy-start(bf16[2,2048,384]{2,1,0:T(8,128)(2,1)} %param.25) | copy-start | bytes 9437188
  780.7 11.1 copy-start.86
  805.3 372.4 %all-to-all-start.1 = ((bf16[16,2,120,2048]{3,2,1,0:T(8,128)(2,1)}), bf16[16,2,120,2048]{3,2,1,0:T(8,128)(2,1)}, u32[]{:S(2)}, u32[]{:S(2)}) async-start(bf16[16,2,120,2048]{3,2,1,0:T(8,128)(2,1)} %copy.231), calls=%async_computation.1 | async-start | bytes 31457280 | tf_op jit(solution)/shard_map/all_to_all | solution.py:200
  811.8 304.6 %all-gather.19.cloned.1.call-start = ((), (), s32[]{:S(2)}) async-start(), calls=%async_computation.17 | async-start | bytes 2359296 | tf_op jit(solution)/shard_map/all_gather | solution.py:214
  814.1 305.1 %copy-start.60 = (s32[4096]{0:T(1024)S(1)}, s32[4096]{0:T(1024)}, u32[]{:S(2)}) copy-start(s32[4096]{0:T(1024)} %copy-done.59) | copy-start | bytes 49156
  1115.5 35.0 %copy-start.44 = (bf16[2048,32]{0,1:T(8,128)(2,1)}, bf16[2048,32]{0,1:T(8,128)(2,1)S(1)}, u32[]{:S(2)}) copy-start(bf16[2048,32]{0,1:T(8,128)(2,1)S(1)} %all_gather.42) | copy-start | bytes 393220
  1152.5 25.2 copy-start.53
  1714.0 17.0 copy-start.34
  1763.6 284.9 %all-to-all-start.3 = ((bf16[16,2,120,2048]{3,2,1,0:T(8,128)(2,1)}), bf16[16,2,120,2048]{3,2,1,0:T(8,128)(2,1)}, u32[]{:S(2)}, u32[]{:S(2)}) async-start(bf16[16,2,120,2048]{3,2,1,0:T(8,128)(2,1)} %copy.234), calls=%async_computation.4 | async-start | bytes 31457280 | tf_op jit(solution)/shard_map/all_to_all | solution.py:243
  1770.1 533.0 %all-reduce.22.cloned.1.call-start = ((), (), s32[]{:S(2)}) async-start(), calls=%async_computation.18 | async-start | bytes 6291456 | tf_op jit(solution)/shard_map/psum | solution.py:265
  2135.4 13.0 copy-start.45
  2156.7 146.4 %copy-start.6 = (f32[384,2048]{1,0:T(8,128)S(1)}, f32[384,2048]{1,0:T(8,128)}, u32[]{:S(2)}) copy-start(f32[384,2048]{1,0:T(8,128)} %copy-done.5) | copy-start | bytes 9437188
  2156.7 146.4 %copy-start.62 = (f32[16,1,128]{2,1,0:T(1,128)S(1)}, f32[16,1,128]{2,1,0:T(1,128)}, u32[]{:S(2)}) copy-start(f32[16,1,128]{2,1,0:T(1,128)} %convert_element_type.280) | copy-start | bytes 24580
  2156.7 146.4 %copy-start.69 = (f32[384]{0:T(512)S(1)}, f32[384]{0:T(512)}, u32[]{:S(2)}) copy-start(f32[384]{0:T(512)} %copy-done.68) | copy-start | bytes 4612
  2156.7 273.9 %all-reduce.24.cloned.1.call-start = ((), (), s32[]{:S(2)}) async-start(), calls=%async_computation.24 | async-start | bytes 3407872 | tf_op jit(solution)/shard_map/psum | solution.py:314
  2159.8 146.7 %copy-start.76 = (f32[384]{0:T(512)S(1)}, f32[384]{0:T(512)}, u32[]{:S(2)}) copy-start(f32[384]{0:T(512)} %copy-done.75) | copy-start | bytes 4612
  2306.5 9.8 slice-start
  2307.5 8.8 slice-start.1
  2376.0 84.3 %reduce-scatter.7.cloned.1.call-start = ((), (), s32[]{:S(2)}) async-start(), calls=%async_computation.16 | async-start | bytes 2359296 | tf_op jit(solution)/shard_map/reduce_scatter | solution.py:209
  2376.1 56.1 %copy-start.4 = (bf16[384,2048]{1,0:T(8,128)(2,1)S(1)}, bf16[384,2048]{1,0:T(8,128)(2,1)}, u32[]{:S(2)}) copy-start(bf16[384,2048]{1,0:T(8,128)(2,1)} %all-gather.9.cloned.1.call-done) | copy-start | bytes 4718596
  2376.1 56.1 %copy-start.56 = (f32[16,1,128]{2,1,0:T(1,128)S(1)}, f32[16,1,128]{2,1,0:T(1,128)}, u32[]{:S(2)}) copy-start(f32[16,1,128]{2,1,0:T(1,128)} %copy-done.55) | copy-start | bytes 24580
  2376.1 56.1 %copy-start.65 = (f32[384]{0:T(512)S(1)}, f32[384]{0:T(512)}, u32[]{:S(2)}) copy-start(f32[384]{0:T(512)} %copy-done.64) | copy-start | bytes 4612
  2382.6 195.3 %reduce-scatter.17.cloned.1.call-start = ((), (), s32[]{:S(2)}) async-start(), calls=%async_computation.23 | async-start | bytes 278528 | tf_op jit(solution)/shard_map/reduce_scatter | solution.py:342
  2432.2 152.4 %reduce-scatter.11.cloned.1.call-start = ((), (), s32[]{:S(2)}) async-start(), calls=%async_computation.20 | async-start | bytes 2228224 | tf_op jit(solution)/shard_map/reduce_scatter | solution.py:336
  2434.6 215.1 %reduce-scatter.13.cloned.1.call-start = ((), (), s32[]{:S(2)}) async-start(), calls=%async_computation.21 | async-start | bytes 2228224 | tf_op jit(solution)/shard_map/reduce_scatter | solution.py:337
  2436.8 393.4 %reduce-scatter.15.cloned.1.call-start = ((), (), s32[]{:S(2)}) async-start(), calls=%async_computation.22 | async-start | bytes 17825792 | tf_op jit(solution)/shard_map/reduce_scatter | solution.py:338
  2447.0 564.3 %reduce-scatter.9.cloned.1.call-start = ((), (), s32[]{:S(2)}) async-start(), calls=%async_computation.19 | async-start | bytes 17825792 | tf_op jit(solution)/shard_map/reduce_scatter | solution.py:335
  2463.1 12.1 copy-start.38
  2475.2 14.0 copy-start.18
  2489.2 14.3 copy-start.83
  2489.2 14.3 copy-start.84
  2489.2 19.2 copy-start.43
  2573.9 437.4 %copy-start.1 = (bf16[2,384,2048]{2,1,0:T(8,128)(2,1)S(1)}, bf16[2,384,2048]{2,1,0:T(8,128)(2,1)}, u32[]{:S(2)}) copy-start(bf16[2,384,2048]{2,1,0:T(8,128)(2,1)} %param.27) | copy-start | bytes 9437188
  (60 other events, 204.2 us)
Sparse Core Ops, SparseCore 0:
  9.5 29.8 all-gather.8
  41.6 37.8 all-gather.12
  81.7 36.8 all-gather.10
  120.5 73.2 all-gather.14
  195.8 76.2 all-gather.16
  281.3 83.9 all-reduce.19
  814.1 27.5 all-gather.18
  2156.8 146.2 all-reduce.21
  2376.1 54.3 all-reduce.23
  2433.2 26.1 reduce-scatter.6
  2463.5 55.7 reduce-scatter.16
  2523.5 60.9 reduce-scatter.10
  2588.8 60.7 reduce-scatter.12
  2654.2 176.0 reduce-scatter.14
  2834.8 176.4 reduce-scatter.8
where the time goes:
time: 3020 us
  blocking collectives  1170 us (39%)
  waiting for transfers between devices  1120 us (37%)
  local copies, waits for them, and re-layouts  392 us (13%)
  matrix products  226 us (7%)
  other arithmetic  79.5 us (3%)
    all_to_all x1, blocking collectives, on_device(): lax.all_to_all(grad_send, 'dp', split_axis=0, concat_axis=0, tiled=True)  390 us
    all_to_all x1, blocking collectives, on_device(): lax.all_to_all(send_rows, 'dp', split_axis=0, concat_axis=0, tiled=True)  346 us
    all_gather x1, blocking collectives, gather_dense(): lax.all_gather(router_weight, 'dp', axis=0, tiled=True)  301 us
    all_to_all x1, waiting for transfers between devices, on_device(): lax.all_to_all(grad_inputs.astype(jnp.bfloat16), 'dp', split_axis=0, conc...  278 us
    reduce_scatter x1, waiting for transfers between devices, on_device(): lax.psum_scatter(q_grad, 'dp', scatter_dimension=0, tiled=True)  181 us
    reduce_scatter x1, waiting for transfers between devices, on_device(): lax.psum_scatter(o_grad, 'dp', scatter_dimension=1, tiled=True)  181 us
    psum x1, waiting for transfers between devices, on_device(): ffn_back = lax.psum(grad_ffn, 'tensor')  143 us
    gather x8, local copies, waits for them, and re-layouts, on_device(): returned[pair_rows[:, column]].astype(jnp.float32)  101 us
  transfers between devices with their start and end apart: 17, of which 12 were waited for; matrix products, arithmetic and copies ran while one was open for 7% of the time, Pallas kernels for 0%

commit v1 on v0

v1 whole, which is shorter than its diff:
```python
import jax
import jax.numpy as jnp
from jax import lax
from jax.sharding import PartitionSpec as P

HEAD = 128
EPS = 1e-06
THETA = 1000000.0
BF = jnp.bfloat16
F32 = jnp.float32


def dot(a, b, ca, cb):
    return lax.dot_general(a, b, (((ca,), (cb,)), ((), ())), preferred_element_type=F32)


def rms(v, gain):
    return v * lax.rsqrt(jnp.mean(v * v, axis=-1, keepdims=True) + EPS) * gain


def rms_back(v, gain, u):
    inv = lax.rsqrt(jnp.mean(v * v, axis=-1, keepdims=True) + EPS)
    ug = u * gain
    grad = ug * inv - v * (jnp.mean(ug * v, axis=-1, keepdims=True) * inv * inv * inv)
    return grad, u * v * inv


def rope(v, cos, sin):
    a, b = v[..., : HEAD // 2], v[..., HEAD // 2 :]
    return jnp.concatenate([a * cos - b * sin, b * cos + a * sin], axis=-1)


def rope_back(v, cos, sin):
    a, b = v[..., : HEAD // 2], v[..., HEAD // 2 :]
    return jnp.concatenate([a * cos + b * sin, b * cos - a * sin], axis=-1)


def rope_tables(count):
    inverse = THETA ** (-(jnp.arange(HEAD // 2, dtype=F32) * 2.0 / HEAD))
    angles = jnp.arange(count, dtype=F32)[:, None] * inverse[None, :]
    return jnp.cos(angles)[:, None, :], jnp.sin(angles)[:, None, :]


def split2(v):
    high = v.astype(BF)
    return high, (v - high.astype(F32)).astype(BF)


def gather_dp(v):
    return lax.all_gather(v, "dp", axis=0, tiled=True)


def gather_all(v):
    return lax.all_gather(v, ("dp", "tensor"), axis=0, tiled=True)


def scatter_all(v):
    return lax.psum_scatter(v, ("dp", "tensor"), scatter_dimension=0, tiled=True)


def scatter_dp(v):
    return lax.psum_scatter(v, "dp", scatter_dimension=0, tiled=True)


def pieces(width, dp, seq):
    count = 1 if dp * seq <= 8192 else 4
    step = width // count // 128 * 128
    edges = [step * i for i in range(count)] + [width]
    return list(zip(edges[:-1], edges[1:]))


def after(v, earlier):
    return v if earlier is None else lax.optimization_barrier((v, earlier))[0]


def dispatch(pick, own, dp, seq, earlier):
    blocks = []
    for low, high in pieces(own.shape[1], dp, seq):
        every = gather_all(after(own[:, low:high], earlier)).reshape(dp, seq, high - low)
        block = jnp.einsum("gest,gtd->gesd", pick, every, preferred_element_type=F32).astype(BF)
        blocks.append(block)
        earlier = block if len(pieces(own.shape[1], dp, seq)) > 1 else None
    return jnp.concatenate(blocks, axis=3)


def combine(pick, rows, dp, seq, earlier):
    blocks = []
    for low, high in pieces(rows.shape[3], dp, seq):
        tok = jnp.einsum(
            "gest,gesd->gtd",
            pick,
            after(rows[:, :, :, low:high], earlier),
            preferred_element_type=F32,
        ).astype(BF)
        blocks.append(scatter_all(tok.reshape(dp * seq, high - low)))
        earlier = blocks[-1] if len(pieces(rows.shape[3], dp, seq)) > 1 else None
    return jnp.concatenate(blocks, axis=1).astype(F32)


def pad_to(v, width):
    return jnp.pad(v, ((0, 0), (0, width - v.shape[1])))


def lanes(count):
    return -(-count // 128) * 128


def on_device(
    tokens,
    attn_gain,
    q_weight,
    key_matrix,
    value_matrix,
    o_weight,
    query_norm_gain,
    k_gain,
    ffn_gain,
    router_weight,
    gate_weight,
    up_weight,
    down_weight,
    expert_ids,
    cotangent,
):
    dp = lax.axis_size("dp")
    tensor = lax.axis_size("tensor")
    dp_at = lax.axis_index("dp")
    own, width = tokens.shape
    seq = expert_ids.shape[0]
    begin = lax.axis_index("tensor") * own
    local = gate_weight.shape[0]
    experts = local * dp
    slots = 10 * seq * expert_ids.shape[1] // (8 * experts)
    slots = -(-slots // 16) * 16
    shard = q_weight.shape[0]
    gshard = query_norm_gain.shape[0]
    hq = q_weight.shape[1] // HEAD
    hk = key_matrix.shape[1] // HEAD
    group = hq // hk
    qkv_width = (hq + 2 * hk) * HEAD

    arange_e = jnp.arange(experts, dtype=jnp.int32)
    own_ids = lax.dynamic_slice_in_dim(expert_ids, begin, own, 0)
    own_mask = jnp.any(own_ids[:, :, None] == arange_e[None, None, :], axis=1)

    gain_rows = jnp.stack(
        [
            attn_gain,
            ffn_gain,
            jnp.pad(query_norm_gain, (0, shard - gshard)),
            jnp.pad(k_gain, (0, shard - gshard)),
        ],
        axis=1,
    )
    small = pad_to(jnp.concatenate([router_weight, gain_rows], axis=1), lanes(experts + 4))
    all_in = gather_dp(jnp.concatenate([q_weight, key_matrix, value_matrix, small], axis=1))
    layer_in = lax.all_gather(tokens, "tensor", axis=0, tiled=True)
    o_t = gather_dp(o_weight.T)
    mask_all = gather_all(pad_to(own_mask.astype(BF), lanes(experts))).reshape(dp, seq, -1)

    w_qkv = all_in[:, :qkv_width]
    router = all_in[:, qkv_width : qkv_width + experts]
    gains = all_in[:, qkv_width + experts : qkv_width + experts + 4].astype(F32)
    attn_gain32 = gains[:, 0]
    ffn_gain32 = gains[:, 1]
    q_gain32 = gains[:, 2].reshape(dp, shard)[:, :gshard].reshape(-1)
    k_gain32 = gains[:, 3].reshape(dp, shard)[:, :gshard].reshape(-1)

    residual = layer_in.astype(F32)
    normed = rms(residual, attn_gain32).astype(BF)
    qkv = dot(normed, w_qkv, 1, 0)
    cos, sin = rope_tables(seq)
    q_raw = qkv[:, : hq * HEAD].reshape(seq, hq, HEAD)
    k_raw = qkv[:, hq * HEAD : (hq + hk) * HEAD].reshape(seq, hk, HEAD)
    v_low = qkv[:, (hq + hk) * HEAD :].astype(BF).reshape(seq, hk, HEAD)
    q_low = rope(rms(q_raw, q_gain32), cos, sin).astype(BF).reshape(seq, hk, group, HEAD)
    k_low = rope(rms(k_raw, k_gain32), cos, sin).astype(BF)
    causal = jnp.arange(seq)[:, None] >= jnp.arange(seq)[None, :]
    scale = HEAD ** (-0.5)
    scores = jnp.einsum("qhgd,khd->hgqk", q_low, k_low, preferred_element_type=F32) * scale
    expo = jnp.where(causal, jnp.exp(scores), 0.0)
    total = jnp.sum(expo, axis=-1, keepdims=True)
    probs = expo / total
    context = jnp.einsum("hgqk,khd->qhgd", probs.astype(BF), v_low, preferred_element_type=F32)
    context = context.reshape(seq, hq * HEAD).astype(BF)
    attn_part = dot(context, o_t, 1, 1).astype(BF)
    attn_own = lax.psum_scatter(attn_part, "tensor", scatter_dimension=0, tiled=True)
    hidden = tokens.astype(F32) + attn_own.astype(F32)

    ffn_in = rms(hidden, ffn_gain32).astype(BF)
    logits = dot(ffn_in, router, 1, 0)
    chosen = jnp.where(own_mask, jnp.exp(logits), 0.0)
    gates = chosen / jnp.sum(chosen, axis=1, keepdims=True)
    gate_high, gate_low = split2(gates)
    gate_x = pad_to(jnp.concatenate([gate_high, gate_low], axis=1), lanes(2 * experts))
    gate_all = gather_all(gate_x).reshape(dp, seq, -1)

    mask = lax.dynamic_slice_in_dim(mask_all, dp_at * local, local, 2)
    before = (jnp.arange(seq)[:, None] > jnp.arange(seq)[None, :]).astype(BF)
    rank = jnp.einsum("ab,gbe->gea", before, mask, preferred_element_type=F32)
    rank = jnp.where(jnp.swapaxes(mask, 1, 2) > 0, rank, -1.0)
    pick = (rank[:, :, None, :] == jnp.arange(slots, dtype=F32)[None, None, :, None]).astype(BF)

    cots = dispatch(pick, cotangent, dp, seq, None)
    rows = dispatch(pick, ffn_in, dp, seq, None if dp * seq <= 8192 else cots)
    gate_tok = lax.dynamic_slice_in_dim(gate_all, dp_at * local, local, 2).astype(
        F32
    ) + lax.dynamic_slice_in_dim(gate_all, experts + dp_at * local, local, 2).astype(F32)
    gate_slot = jnp.sum(pick.astype(F32) * jnp.swapaxes(gate_tok, 1, 2)[:, :, None, :], axis=3)

    g_proj = jnp.einsum("gesd,edf->gesf", rows, gate_weight, preferred_element_type=F32)
    u_proj = jnp.einsum("gesd,edf->gesf", rows, up_weight, preferred_element_type=F32)
    d_act = jnp.einsum("gesd,efd->gesf", cots, down_weight, preferred_element_type=F32)
    sig = 1.0 / (1.0 + jnp.exp(-g_proj))
    silu = g_proj * sig
    act = silu * u_proj
    scaled = (act * gate_slot[..., None]).astype(BF)
    d_gate_slot = jnp.sum(act * d_act, axis=3)
    d_act = d_act * gate_slot[..., None]
    d_g = (d_act * u_proj * sig * (1.0 + g_proj * (1.0 - sig))).astype(BF)
    d_u = (d_act * silu).astype(BF)
    d_rows = (
        jnp.einsum("gesf,edf->gesd", d_g, gate_weight, preferred_element_type=F32)
        + jnp.einsum("gesf,edf->gesd", d_u, up_weight, preferred_element_type=F32)
    ).astype(BF)
    dg_high, dg_low = split2(d_gate_slot)
    column = jnp.arange(lanes(2 * experts))
    mine = dp_at * local + jnp.arange(local)
    high_col = (column[None, :] == mine[:, None])[None, :, None, :]
    low_col = (column[None, :] == experts + mine[:, None])[None, :, None, :]
    extra = jnp.where(high_col, dg_high[..., None], jnp.where(low_col, dg_low[..., None], 0.0))
    d_rows = jnp.concatenate([d_rows, extra.astype(BF)], axis=3)
    d_sum = combine(pick, d_rows, dp, seq, None)

    y_rows = jnp.einsum("gesf,efd->gesd", scaled, down_weight, preferred_element_type=F32)
    y_sum = combine(pick, y_rows.astype(BF), dp, seq, None if dp * seq <= 8192 else d_sum)
    output = (hidden + y_sum).astype(BF)
    down_grad = jnp.einsum("gesf,gesd->efd", scaled, cots, preferred_element_type=F32)
    gate_grad = jnp.einsum("gesd,gesf->edf", rows, d_g, preferred_element_type=F32)
    up_grad = jnp.einsum("gesd,gesf->edf", rows, d_u, preferred_element_type=F32)

    d_gates = d_sum[:, width : width + experts] + d_sum[:, width + experts : width + 2 * experts]
    d_logits = gates * (d_gates - jnp.sum(gates * d_gates, axis=1, keepdims=True))
    d_high, d_low = split2(d_logits)
    d_ffn = d_sum[:, :width] + dot(d_high, router, 1, 1) + dot(d_low, router, 1, 1)
    router_part = dot(ffn_in, d_high, 0, 0) + dot(ffn_in, d_low, 0, 0)
    d_hidden, ffn_gain_rows = rms_back(hidden, ffn_gain32, d_ffn)
    ffn_gain_part = jnp.sum(ffn_gain_rows, axis=0)
    d_hidden = d_hidden + cotangent.astype(F32)
    d_attn = lax.all_gather(d_hidden.astype(BF), "tensor", axis=0, tiled=True)

    o_part = dot(d_attn, context, 0, 0).astype(BF)
    d_context = dot(d_attn, o_t, 1, 0).astype(BF).reshape(seq, hk, group, HEAD)
    d_probs = jnp.einsum("qhgd,khd->hgqk", d_context, v_low, preferred_element_type=F32)
    d_values = jnp.einsum("hgqk,qhgd->khd", probs.astype(BF), d_context, preferred_element_type=F32)
    d_scores = probs * (d_probs - jnp.sum(probs * d_probs, axis=-1, keepdims=True))
    d_scores = d_scores.astype(BF)
    d_q = jnp.einsum("hgqk,khd->qhgd", d_scores, k_low, preferred_element_type=F32) * scale
    d_k = jnp.einsum("hgqk,qhgd->khd", d_scores, q_low, preferred_element_type=F32) * scale
    d_q_raw, q_gain_rows = rms_back(q_raw, q_gain32, rope_back(d_q.reshape(seq, hq, HEAD), cos, sin))
    d_k_raw, k_gain_rows = rms_back(k_raw, k_gain32, rope_back(d_k, cos, sin))
    d_qkv = jnp.concatenate(
        [
            d_q_raw.reshape(seq, hq * HEAD).astype(BF),
            d_k_raw.reshape(seq, hk * HEAD).astype(BF),
            d_values.reshape(seq, hk * HEAD).astype(BF),
        ],
        axis=1,
    )
    d_normed = dot(d_qkv, w_qkv, 1, 1).astype(BF)
    d_normed = lax.psum_scatter(d_normed, "tensor", scatter_dimension=0, tiled=True).astype(F32)
    qkv_part = dot(normed, d_qkv, 0, 0).astype(BF)
    d_tokens, attn_gain_rows = rms_back(tokens.astype(F32), attn_gain32, d_normed)
    tokens_grad = d_tokens + d_hidden

    o_sum = scatter_dp(o_part).astype(F32)
    qkv_sum = scatter_dp(qkv_part).astype(F32)
    spread = lambda v: jnp.pad(v.reshape(dp, gshard), ((0, 0), (0, shard - gshard))).reshape(-1)
    small_part = jnp.concatenate(
        [
            router_part,
            jnp.stack(
                [
                    jnp.sum(attn_gain_rows, axis=0),
                    ffn_gain_part,
                    spread(jnp.sum(q_gain_rows, axis=(0, 1))),
                    spread(jnp.sum(k_gain_rows, axis=(0, 1))),
                ],
                axis=1,
            ),
        ],
        axis=1,
    )
    small_part = pad_to(small_part, lanes(experts + 4))
    small_sum = lax.psum(scatter_dp(small_part), "tensor")
    return (
        output,
        tokens_grad,
        small_sum[:, experts],
        qkv_sum[:, : hq * HEAD],
        qkv_sum[:, hq * HEAD : (hq + hk) * HEAD],
        qkv_sum[:, (hq + hk) * HEAD :],
        o_sum.T,
        small_sum[:gshard, experts + 2],
        small_sum[:gshard, experts + 3],
        small_sum[:, experts + 1],
        small_sum[:, :experts],
        gate_grad,
        up_grad,
        down_grad,
    )


def solution(mesh):
    rows = P(("dp", "tensor"), None)
    both = P("dp", "tensor")
    return jax.shard_map(
        on_device,
        mesh=mesh,
        in_specs=(
            rows,
            P("dp"),
            both,
            both,
            both,
            P("tensor", "dp"),
            P("dp"),
            P("dp"),
            P("dp"),
            P("dp", None),
            P("dp", None, "tensor"),
            P("dp", None, "tensor"),
            P("dp", "tensor", None),
            P("dp", None),
            rows,
        ),
        out_specs=(
            rows,
            rows,
            P("dp"),
            both,
            both,
            both,
            P("tensor", "dp"),
            P("dp"),
            P("dp"),
            P("dp"),
            P("dp", None),
            P("dp", None, "tensor"),
            P("dp", None, "tensor"),
            P("dp", "tensor", None),
        ),
        check_vma=False,
    )
```

time: 3020 us -> 1730 us (0.57)
  blocking collectives: 1170 us -> 0 us
  local copies, waits for them, and re-layouts: 392 us -> 74.8 us
  waiting for transfers between devices: 1120 us -> 1260 us
  matrix products: 226 us -> 303 us
    all_to_all x2 -> x0, blocking collectives: 736 us -> none  [the longest x1 390 us: on_device(): lax.all_to_all(grad_send, 'dp', split_axis=0, concat_axis=0, tiled=True)]
    all_gather x3 -> x0, blocking collectives: 337 us -> none  [the longest x1 301 us: gather_dense(): lax.all_gather(router_weight, 'dp', axis=0, tiled=True)]
    all_gather x5 -> x7, waiting for transfers between devices: 163 us -> 484 us  [the longest x4 349 us: gather_all(): return lax.all_gather(v, ('dp', 'tensor'), axis=0, tiled=True)]
    reduce_scatter x6 -> x7, waiting for transfers between devices: 433 us -> 733 us  [the longest x2 435 us: scatter_all(): lax.psum_scatter(v, ('dp', 'tensor'), scatter_dimension=0, tiled=True)]
    gather x23 -> x0, local copies, waits for them, and re-layouts: 290 us -> none  [the longest x8 101 us: on_device(): returned[pair_rows[:, column]].astype(jnp.float32)]
    all_to_all x2 -> x0, waiting for transfers between devices: 278 us -> none  [the longest x1 278 us: on_device(): lax.all_to_all(grad_inputs.astype(jnp.bfloat16), 'dp', split_axis=0, conc...]
    psum x3 -> x1, waiting for transfers between devices: 238 us -> 18.5 us  [on_device(): small_sum = lax.psum(scatter_dp(small_part), 'tensor')]
    unnamed x2 -> x0, blocking collectives: 95.3 us -> none
  transfers between devices with their start and end apart: 17 -> 16, of which waited for: 12 -> 16; matrix products, arithmetic and copies ran while one was open for 7% -> 13% of each run, Pallas kernels for 0% -> 0%
where the time goes in v1:
time: 1730 us; the launch traced here: 1720 us
  waiting for transfers between devices  1260 us (73%)
  matrix products  303 us (18%)
  local copies, waits for them, and re-layouts  74.8 us (4%)
  other arithmetic  64.4 us (4%)
    reduce_scatter x2, waiting for transfers between devices, scatter_all(): lax.psum_scatter(v, ('dp', 'tensor'), scatter_dimension=0, tiled=True)  435 us
    all_gather x4, waiting for transfers between devices, gather_all(): return lax.all_gather(v, ('dp', 'tensor'), axis=0, tiled=True)  349 us
    reduce_scatter x3, waiting for transfers between devices, scatter_dp(): return lax.psum_scatter(v, 'dp', scatter_dimension=0, tiled=True)  264 us
    all_gather x2, waiting for transfers between devices, gather_dp(): return lax.all_gather(v, 'dp', axis=0, tiled=True)  116 us
    dot_general x11, matrix products, dot(): lax.dot_general(a, b, (((ca,), (cb,)), ((), ())), preferred_element_type=...  58.3 us
    dot_general x2, matrix products, dispatch(): jnp.einsum('gest,gtd->gesd', pick, every, preferred_element_type=F32)  44.1 us
    dot_general x2, matrix products, combine(): jnp.einsum('gest,gesd->gtd', pick, after(rows[:, :, :, low:high], earlier...  38 us
  transfers between devices with their start and end apart: 16, of which 16 were waited for; matrix products, arithmetic and copies ran while one was open for 13% of the time, Pallas kernels for 0%

profile of v1, /device:TPU:0, one launch (start us, length us, event | category | flops | bytes accessed | tf_op | source)
XLA Modules:
  0.0 1723.0 jit_solution(10741799119661562667)
XLA Ops:
  15.5 24.9 %all-gather.9.cloned.1.call-done = bf16[384,2048]{1,0:T(8,128)(2,1)} async-done(((bf16[192,2048]{1,0:T(8,128)(2,1)}), bf16[384,2048]{1,0:T(8,128)(2,1)}) %all-gather.9.cloned.1.call-update) | async-done | bytes 1572880 | tf_op jit(solution)/shard_map/all_gather | solution.py:157
  42.7 91.3 %all-gather.11.cloned.1.call-done = bf16[2048,2688]{1,0:T(8,128)(2,1)} async-done(((bf16[128,2688]{1,0:T(8,128)(2,1)}), bf16[2048,2688]{1,0:T(8,128)(2,1)}) %all-gather.11.cloned.1.call-update) | async-done | bytes 11010064 | tf_op jit(solution)/shard_map/all_gather | solution.py:50
  140.2 7.9 fusion.19
  169.8 2.8 multiply_multiply_fusion
  175.9 3.2 fusion.24
  187.2 25.0 %all-gather.13.cloned.1.call-done = bf16[2048,2048]{0,1:T(8,128)(2,1)} async-done(((bf16[128,2048]{0,1:T(8,128)(2,1)}), bf16[2048,2048]{0,1:T(8,128)(2,1)}) %all-gather.13.cloned.1.call-update) | async-done | bytes 8388624 | tf_op jit(solution)/shard_map/all_gather | solution.py:50
  212.1 8.5 convolution_convert_fusion.5
  221.7 23.6 %reduce-scatter.8.cloned.1.call-done = bf16[192,2048]{1,0:T(8,128)(2,1)} async-done(((bf16[384,2048]{1,0:T(8,128)(2,1)}), bf16[192,2048]{1,0:T(8,128)(2,1)}) %reduce-scatter.8.cloned.1.call-update) | async-done | bytes 786448 | tf_op jit(solution)/shard_map/reduce_scatter | solution.py:187
  253.9 33.2 %all-gather.15.cloned.1.call-done = bf16[6144,128]{1,0:T(8,128)(2,1)} async-done(((bf16[192,128]{1,0:T(8,128)(2,1)}), bf16[6144,128]{1,0:T(8,128)(2,1)}) %all-gather.15.cloned.1.call-update) | async-done | bytes 1572880 | tf_op jit(solution)/shard_map/all_gather | solution.py:54
  287.1 3.1 constant_dynamic-slice_fusion
  292.1 52.3 %all-gather.19.cloned.1.call-done = bf16[6144,128]{1,0:T(8,128)(2,1)} async-done(((bf16[192,128]{1,0:T(8,128)(2,1)}), bf16[6144,128]{1,0:T(8,128)(2,1)}) %all-gather.19.cloned.1.call-update) | async-done | bytes 1572880 | tf_op jit(solution)/shard_map/all_gather | solution.py:54
  344.4 4.4 add_bitcast_fusion
  351.2 3.9 multiply_reduce_fusion
  355.1 144.9 %all-gather.21.cloned.1.call-done = bf16[6144,2048]{1,0:T(8,128)(2,1)} async-done(((bf16[192,2048]{1,0:T(8,128)(2,1)}), bf16[6144,2048]{1,0:T(8,128)(2,1)}) %all-gather.21.cloned.1.call-update) | async-done | bytes 25165840 | tf_op jit(solution)/shard_map/all_gather | solution.py:54
  500.0 22.1 %convolution_convert_fusion = bf16[16,2,128,2048]{3,2,1,0:T(8,128)(2,1)} fusion(bf16[16,384,2048,1]{2,1,3,0:T(8,128)(2,1)} %bitcast.299, f32[16,2,384]{2,1,0:T(2,128)S(1)} %copy.344), kind=kOutput, calls=%fused_computation.17 | convolution fusion | flops 6452412416 | bytes 41992192 | tf_op jit(solution)/shard_map/gest,gtd->gesd/dot_general | solution.py:80
  522.2 14.2 fusion.8
  536.4 119.0 %all-gather.17.cloned.1.call-done = bf16[6144,2048]{1,0:T(8,128)(2,1)} async-done(((bf16[192,2048]{1,0:T(8,128)(2,1)}), bf16[6144,2048]{1,0:T(8,128)(2,1)}) %all-gather.17.cloned.1.call-update) | async-done | bytes 25165840 | tf_op jit(solution)/shard_map/all_gather | solution.py:54
  655.4 21.9 %convolution_convert_fusion.1 = bf16[16,2,128,2048]{3,2,1,0:T(8,128)(2,1)} fusion(bf16[16,384,2048,1]{2,1,3,0:T(8,128)(2,1)} %bitcast.300, f32[16,2,384]{2,1,0:T(2,128)S(1)} %copy.344), kind=kOutput, calls=%fused_computation.18 | convolution fusion | flops 6452412416 | bytes 41992192 | tf_op jit(solution)/shard_map/gest,gtd->gesd/dot_general | solution.py:80
  677.3 14.6 fusion.12
  691.9 19.8 %fusion.28 = (bf16[16,2,128,384]{3,2,0,1:T(8,128)(2,1)}, f32[16,2,128]{2,0,1:T(8,128)S(1)}, bf16[16,2,128,384]{3,2,0,1:T(8,128)(2,1)}, bf16[16,2,128,384]{3,2,0,1:T(8,128)(2,1)}) fusion(f32[2,16,128,384]{3,2,1,0:T(8,128)} %fusion.12, f32[2,16,128,384]{3,2,1,0:T(8,128)} %fusion.8, f32[16,2,128]{2,0,1:T(8,128)S(1)} %copy.351, ...), kind=kOutput, calls=%fused_computation.41 | convolution fusion | flops 6472331264 | bytes 41975808 | tf_op jit(solution)/shard_map/gesd,edf->gesf/dot_general | solution.py:212
  711.7 18.0 %fusion.49 = f32[2,16,128,2048]{3,2,0,1:T(8,128)} fusion(bf16[2,2048,384]{2,1,0:T(8,128)(2,1)} %param.25, bf16[16,2,128,384]{3,2,0,1:T(8,128)(2,1)} %get-tuple-element.139), kind=kOutput, calls=%fused_computation.76 | convolution fusion | flops 6442450944 | bytes 39845888 | tf_op jit(solution)/shard_map/gesf,edf->gesd/dot_general | solution.py:223
  729.7 19.3 %fusion.3 = bf16[16,2,128,2048]{3,2,1,0:T(8,128)(2,1)} fusion(f32[2,16,128,2048]{3,2,0,1:T(8,128)} %fusion.49, bf16[2,2048,384]{2,1,0:T(8,128)(2,1)S(1)} %copy-done, bf16[16,2,128,384]{3,2,0,1:T(8,128)(2,1)S(1)} %copy-done.28), kind=kOutput, calls=%fused_computation.6 | convolution fusion | flops 6459228160 | bytes 56623104 | tf_op jit(solution)/shard_map/gesf,edf->gesd/dot_general | solution.py:224
  750.3 20.5 %bitcast_convert_fusion = bf16[16,384,2176]{2,1,0:T(8,128)(2,1)} fusion(bf16[16,2,128,128]{3,2,1,0:T(8,128)(2,1)S(1)} %select_select_fusion, bf16[16,2,128,2048]{3,2,1,0:T(8,128)(2,1)} %fusion.3, f32[16,2,384]{2,1,0:T(2,128)S(1)} %copy.344), kind=kOutput, calls=%fused_computation | convolution fusion | flops 6895697920 | bytes 44613632 | tf_op jit(solution)/shard_map/gest,gesd->gtd/dot_general | solution.py:89
  770.9 251.9 %reduce-scatter.12.cloned.1.call-done = bf16[192,2176]{1,0:T(8,128)(2,1)} async-done(((bf16[6144,2176]{1,0:T(8,128)(2,1)}), bf16[192,2176]{1,0:T(8,128)(2,1)}) %reduce-scatter.12.cloned.1.call-update) | async-done | bytes 835600 | tf_op jit(solution)/shard_map/reduce_scatter | solution.py:58
  1031.0 7.2 copy.374
  1038.8 18.1 %all-gather.23.cloned.1.call-done = bf16[384,2048]{1,0:T(8,128)(2,1)} async-done(((bf16[192,2048]{1,0:T(8,128)(2,1)}), bf16[384,2048]{1,0:T(8,128)(2,1)}) %all-gather.23.cloned.1.call-update) | async-done | bytes 1572880 | tf_op jit(solution)/shard_map/all_gather | solution.py:250
  1056.9 7.3 fusion.73
  1065.2 7.0 fusion.14
  1072.3 2.8 fusion.16
  1088.1 2.6 copy.416
  1090.8 3.6 multiply_add_fusion
  1094.5 3.2 multiply_reduce_fusion.1
  1105.7 5.0 fusion.42
  1111.9 9.5 fusion.57
  1121.6 14.7 fusion.149
  1137.2 10.6 reduce-scatter.14.cloned.1.call-done
  1150.6 17.4 %bitcast_convert_fusion.1 = bf16[16,384,2048]{2,1,0:T(8,128)(2,1)} fusion(f32[16,2,384]{2,1,0:T(2,128)S(1)} %copy-done.41, bf16[16,2,128,2048]{3,2,1,0:T(8,128)(2,1)} %fusion.149), kind=kOutput, calls=%fused_computation.1 | convolution fusion | flops 6456606720 | bytes 41992192 | tf_op jit(solution)/shard_map/gest,gesd->gtd/dot_general | solution.py:89
  1168.2 41.5 %reduce-scatter.16.cloned.1.call-done = f32[128,128]{0,1:T(8,128)} async-done(((f32[2048,128]{0,1:T(8,128)}), f32[128,128]{0,1:T(8,128)}) %reduce-scatter.16.cloned.1.call-update) | async-done | bytes 65552 | tf_op jit(solution)/shard_map/reduce_scatter | solution.py:62
  1209.8 8.3 convolution_convert_fusion.3
  1219.4 10.5 convolution_convert_fusion.2
  1230.0 14.3 fusion.34
  1244.3 15.2 convolution_bitcast_fusion.1
  1259.5 15.6 convolution_bitcast_fusion
  1275.2 183.0 %reduce-scatter.10.cloned.1.call-done = bf16[192,2048]{1,0:T(8,128)(2,1)} async-done(((bf16[6144,2048]{1,0:T(8,128)(2,1)}), bf16[192,2048]{1,0:T(8,128)(2,1)}) %reduce-scatter.10.cloned.1.call-update) | async-done | bytes 786448 | tf_op jit(solution)/shard_map/reduce_scatter | solution.py:58
  1458.2 4.2 fusion.66
  1462.4 18.5 %all-reduce.10.cloned.1.call-done = f32[128,128]{0,1:T(8,128)} async-done(((f32[128,128]{0,1:T(8,128)}), f32[128,128]{0,1:T(8,128)}) %all-reduce.10.cloned.1.call-update) | async-done | bytes 65552 | tf_op jit(solution)/shard_map/psum | solution.py:295
  1484.9 103.4 %reduce-scatter.20.cloned.1.call-done = bf16[128,2048]{1,0:T(8,128)(2,1)} async-done(((bf16[2048,2048]{1,0:T(8,128)(2,1)}), bf16[128,2048]{1,0:T(8,128)(2,1)}) %reduce-scatter.20.cloned.1.call-update) | async-done | bytes 524304 | tf_op jit(solution)/shard_map/reduce_scatter | solution.py:62
  1593.0 118.6 %reduce-scatter.18.cloned.1.call-done = bf16[128,2560]{1,0:T(8,128)(2,1)} async-done(((bf16[2048,2560]{1,0:T(8,128)(2,1)}), bf16[128,2560]{1,0:T(8,128)(2,1)}) %reduce-scatter.18.cloned.1.call-update) | async-done | bytes 655376 | tf_op jit(solution)/shard_map/reduce_scatter | solution.py:62
  (306 shorter events, 113.1 us)
Async XLA Ops:
  8.0 683.9 %copy-start = (bf16[2,2048,384]{2,1,0:T(8,128)(2,1)S(1)}, bf16[2,2048,384]{2,1,0:T(8,128)(2,1)}, u32[]{:S(2)}) copy-start(bf16[2,2048,384]{2,1,0:T(8,128)(2,1)} %param.26) | copy-start | bytes 9437188
  8.0 32.3 %all-gather.9.cloned.1.call-start = ((), (), s32[]{:S(2)}) async-start(), calls=%async_computation.7 | async-start | bytes 2359296 | tf_op jit(solution)/shard_map/all_gather | solution.py:157
  8.8 125.2 %all-gather.11.cloned.1.call-start = ((), (), s32[]{:S(2)}) async-start(), calls=%async_computation.8 | async-start | bytes 11698176 | tf_op jit(solution)/shard_map/all_gather | solution.py:50
  13.2 198.9 %all-gather.13.cloned.1.call-start = ((), (), s32[]{:S(2)}) async-start(), calls=%async_computation.9 | async-start | bytes 8912896 | tf_op jit(solution)/shard_map/all_gather | solution.py:50
  14.0 231.4 %reduce-scatter.8.cloned.1.call-start = ((), (), s32[]{:S(2)}) async-start(), calls=%async_computation.10 | async-start | bytes 2359296 | tf_op jit(solution)/shard_map/reduce_scatter | solution.py:187
  15.5 160.2 %copy-start.23 = (f32[384,64]{1,0:T(8,128)}, f32[384,64]{1,0:T(8,128)S(1)}, u32[]{:S(2)}) copy-start(f32[384,64]{1,0:T(8,128)S(1)} %get-tuple-element.171) | copy-start | bytes 294916
  15.5 160.2 %copy-start.25 = (f32[384,64]{1,0:T(8,128)}, f32[384,64]{1,0:T(8,128)S(1)}, u32[]{:S(2)}) copy-start(f32[384,64]{1,0:T(8,128)S(1)} %get-tuple-element.172) | copy-start | bytes 294916
  137.6 10.5 copy-start.58
  137.6 891.0 %copy-start.51 = (f32[2048]{0:T(1024)}, f32[2048]{0:T(1024)S(1)}, u32[]{:S(2)}) copy-start(f32[2048]{0:T(1024)S(1)} %get-tuple-element.130) | copy-start | bytes 24580
  159.3 15.4 copy-start.62
  212.1 8.6 copy-start.72
  220.7 66.4 %all-gather.15.cloned.1.call-start = ((), (), s32[]{:S(2)}) async-start(), calls=%async_computation.11 | async-start | bytes 1622016 | tf_op jit(solution)/shard_map/all_gather | solution.py:54
  221.6 122.8 %all-gather.19.cloned.1.call-start = ((), (), s32[]{:S(2)}) async-start(), calls=%async_computation.13 | async-start | bytes 1622016 | tf_op jit(solution)/shard_map/all_gather | solution.py:54
  247.0 781.5 %copy-start.64 = (f32[192]{0:T(256)}, f32[192]{0:T(256)S(1)}, u32[]{:S(2)}) copy-start(f32[192]{0:T(256)S(1)} %add_rsqrt_fusion.4) | copy-start | bytes 2308
  252.2 247.8 %all-gather.21.cloned.1.call-start = ((), (), s32[]{:S(2)}) async-start(), calls=%async_computation.15 | async-start | bytes 25952256 | tf_op jit(solution)/shard_map/all_gather | solution.py:54
  252.7 402.7 %all-gather.17.cloned.1.call-start = ((), (), s32[]{:S(2)}) async-start(), calls=%async_computation.12 | async-start | bytes 25952256 | tf_op jit(solution)/shard_map/all_gather | solution.py:54
  253.5 769.3 %reduce-scatter.12.cloned.1.call-start = ((), (), s32[]{:S(2)}) async-start(), calls=%async_computation.16 | async-start | bytes 27574272 | tf_op jit(solution)/shard_map/reduce_scatter | solution.py:58
  292.1 458.2 %copy-start.40 = (f32[16,2,384]{2,1,0:T(2,128)}, f32[16,2,384]{2,1,0:T(2,128)S(1)}, u32[]{:S(2)}) copy-start(f32[16,2,384]{2,1,0:T(2,128)S(1)} %copy.344) | copy-start | bytes 147460
  500.0 22.1 %copy-start.78 = (bf16[2,384,2048]{2,1,0:T(8,128)(2,1)S(1)}, bf16[2,384,2048]{2,1,0:T(8,128)(2,1)}, u32[]{:S(2)}) copy-start(bf16[2,384,2048]{2,1,0:T(8,128)(2,1)} %param.27) | copy-start | bytes 9437188
  655.4 21.9 %copy-start.33 = (bf16[2,2048,384]{2,1,0:T(8,128)(2,1)S(1)}, bf16[2,2048,384]{2,1,0:T(8,128)(2,1)}, u32[]{:S(2)}) copy-start(bf16[2,2048,384]{2,1,0:T(8,128)(2,1)} %param.25) | copy-start | bytes 9437188
  711.7 18.0 %copy-start.28 = (bf16[16,2,128,384]{3,2,0,1:T(8,128)(2,1)S(1)}, bf16[16,2,128,384]{3,2,0,1:T(8,128)(2,1)}, u32[]{:S(2)}) copy-start(bf16[16,2,128,384]{3,2,0,1:T(8,128)(2,1)} %get-tuple-element.141) | copy-start | bytes 9437188
  770.8 255.1 %copy-start.5 = (bf16[192,2048]{1,0:T(8,128)(2,1)S(1)}, bf16[192,2048]{1,0:T(8,128)(2,1)}, u32[]{:S(2)}) copy-start(bf16[192,2048]{1,0:T(8,128)(2,1)} %param.15) | copy-start | bytes 2359300
  770.9 255.1 %copy-start.8 = (bf16[192,2048]{1,0:T(8,128)(2,1)S(1)}, bf16[192,2048]{1,0:T(8,128)(2,1)}, u32[]{:S(2)}) copy-start(bf16[192,2048]{1,0:T(8,128)(2,1)} %reduce-scatter.8.cloned.1.call-done) | copy-start | bytes 2359300
  770.9 286.0 %all-gather.23.cloned.1.call-start = ((), (), s32[]{:S(2)}) async-start(), calls=%async_computation.17 | async-start | bytes 2359296 | tf_op jit(solution)/shard_map/all_gather | solution.py:250
  1028.5 9.7 copy-start.10
  1028.5 9.7 copy-start.66
  1030.1 117.7 %reduce-scatter.14.cloned.1.call-start = ((), (), s32[]{:S(2)}) async-start(), calls=%async_computation.18 | async-start | bytes 2359296 | tf_op jit(solution)/shard_map/reduce_scatter | solution.py:271
  1121.5 88.2 %reduce-scatter.16.cloned.1.call-start = ((), (), s32[]{:S(2)}) async-start(), calls=%async_computation.19 | async-start | bytes 1114112 | tf_op jit(solution)/shard_map/reduce_scatter | solution.py:62
  1121.5 14.8 copy-start.68
  1121.5 14.8 copy-start.14
  1121.6 14.8 copy-start.35
  1121.6 15.4 copy-start.77
  1121.6 26.2 %copy-start.59 = (f32[2048]{0:T(1024)S(1)}, f32[2048]{0:T(1024)}, u32[]{:S(2)}) copy-start(f32[2048]{0:T(1024)} %copy-done.58) | copy-start | bytes 24580
  1136.3 11.5 copy-start.6
  1136.6 14.0 copy-start.41
  1150.6 307.6 %reduce-scatter.10.cloned.1.call-start = ((), (), s32[]{:S(2)}) async-start(), calls=%async_computation.14 | async-start | bytes 25952256 | tf_op jit(solution)/shard_map/reduce_scatter | solution.py:58
  1168.1 41.7 %copy-start.38 = (bf16[2,128,8,384]{3,1,2,0:T(8,128)(2,1)S(1)}, bf16[2,128,8,384]{3,1,2,0:T(8,128)(2,1)}, u32[]{:S(2)}) copy-start(bf16[2,128,8,384]{3,1,2,0:T(8,128)(2,1)} %convolution_convert_fusion.6) | copy-start | bytes 4718596
  1168.1 312.8 %all-reduce.10.cloned.1.call-start = ((), (), s32[]{:S(2)}) async-start(), calls=%async_computation.20 | async-start | bytes 131072 | tf_op jit(solution)/shard_map/psum | solution.py:295
  1209.7 378.6 %reduce-scatter.20.cloned.1.call-start = ((), (), s32[]{:S(2)}) async-start(), calls=%async_computation.22 | async-start | bytes 8912896 | tf_op jit(solution)/shard_map/reduce_scatter | solution.py:62
  1218.1 493.5 %reduce-scatter.18.cloned.1.call-start = ((), (), s32[]{:S(2)}) async-start(), calls=%async_computation.21 | async-start | bytes 11141120 | tf_op jit(solution)/shard_map/reduce_scatter | solution.py:62
  1230.0 14.3 copy-start.27
  1244.3 15.2 copy-start.29
  1259.5 198.7 %copy-start.9 = (bf16[192,2048]{1,0:T(8,128)(2,1)S(1)}, bf16[192,2048]{1,0:T(8,128)(2,1)}, u32[]{:S(2)}) copy-start(bf16[192,2048]{1,0:T(8,128)(2,1)} %reduce-scatter.8.cloned.1.call-done) | copy-start | bytes 2359300
  1259.5 198.7 %copy-start.11 = (f32[192,2048]{1,0:T(8,128)S(1)}, f32[192,2048]{1,0:T(8,128)}, u32[]{:S(2)}) copy-start(f32[192,2048]{1,0:T(8,128)} %copy-done.10) | copy-start | bytes 4718596
  1259.5 198.7 %copy-start.52 = (f32[2048]{0:T(1024)S(1)}, f32[2048]{0:T(1024)}, u32[]{:S(2)}) copy-start(f32[2048]{0:T(1024)} %copy-done.51) | copy-start | bytes 24580
  1259.5 198.7 %copy-start.65 = (f32[192]{0:T(256)S(1)}, f32[192]{0:T(256)}, u32[]{:S(2)}) copy-start(f32[192]{0:T(256)} %copy-done.64) | copy-start | bytes 2308
  1259.5 198.7 %copy-start.67 = (f32[192]{0:T(256)S(1)}, f32[192]{0:T(256)}, u32[]{:S(2)}) copy-start(f32[192]{0:T(256)} %copy-done.66) | copy-start | bytes 2308
  1483.5 231.7 %copy-start.1 = (bf16[2,2048,384]{2,1,0:T(8,128)(2,1)S(1)}, bf16[2,2048,384]{2,1,0:T(8,128)(2,1)}, u32[]{:S(2)}) copy-start(bf16[2,2048,384]{2,1,0:T(8,128)(2,1)} %param.26) | copy-start | bytes 9437188
  (52 other events, 172.1 us)
Sparse Core Ops, SparseCore 0:
  10.4 29.9 all-gather.8
  43.2 90.7 all-gather.10
  136.2 75.9 all-gather.12
  220.8 24.4 reduce-scatter.7
  1030.2 26.6 all-gather.22
  1121.6 26.1 reduce-scatter.13
  1152.0 57.6 reduce-scatter.15
  1216.1 242.0 reduce-scatter.9
  1460.4 20.4 all-reduce.9
  1484.8 103.4 reduce-scatter.19
  1592.4 119.1 reduce-scatter.17
Sparse Core Ops, SparseCore 1:
  224.6 62.4 all-gather.14
  290.4 53.9 all-gather.18
  347.2 152.8 all-gather.20
  503.5 151.8 all-gather.16
  770.9 251.8 reduce-scatter.11
